TPU v7x, 512 devices: a whole 4x4x16 slice. The times are simulated.
512 devices in a mesh: row: 32 (over x, y, core), col: 16 (over z).
Axes of the slice: x: 4, y: 4, z: 16, core: 2. Of those that a mesh axis runs over, the one named last changes fastest.
Arguments:
- similarity: float32 [8192, 8192], P('row', 'col'), may hold values from 0.1 to 500
- pattern: int32 [32, 32], P('row', 'col'), may hold values from 0 to 1, as said below
Outputs:
- clustered: float32 [8192, 8192], P('row', 'col')
Inputs may be any that keep to these rules, and one draw needn't show every extreme that they name: `pattern`: every diagonal tile (g, g) is stored.
All inputs are finite; a program needn't handle non-finite values.
Results may differ from a plain program's by a relative error of at most 0.0003.
Values may be sent and summed in bfloat16 or wider, within the bound.
A program may use at most 64 MiB of HBM per device.

v0:
```python
import jax
import jax.numpy as jnp
from jax import lax
from jax.sharding import PartitionSpec as P

TILE = 256


def spread(pattern):
    rows, cols = pattern.shape
    values = pattern.astype(jnp.float32)
    return jnp.broadcast_to(values[:, None, :, None], (rows, TILE, cols, TILE)).reshape(
        rows * TILE, cols * TILE
    )


def tile_sum(left_part, right_part):
    return jnp.dot(left_part, right_part, preferred_element_type=jnp.float32)


def product(operand):
    left = lax.all_gather(operand, "col", axis=1, tiled=True)
    return tile_sum(left, lax.all_gather(operand, "row", axis=0, tiled=True))


def shards(similarity, pattern):
    cells = spread(pattern)
    total_rows = similarity.shape[0] * lax.axis_size("row")
    held = similarity * cells
    start_total = lax.psum(jnp.sum(held, axis=0), "row")
    matrix = held * (total_rows / start_total)[None, :]
    operand = matrix.astype(jnp.bfloat16)
    expanded = product(operand) * cells
    inflated = expanded * expanded
    sums = lax.psum(jnp.sum(inflated, axis=0), "row")
    matrix = inflated * (total_rows / sums)[None, :]
    return matrix


def solution(mesh):
    placed = (P("row", "col"), P("row", "col"))
    return jax.shard_map(
        shards, mesh=mesh, in_specs=placed, out_specs=P("row", "col"), check_vma=False
    )
```

profile of v0, /device:TPU:32, one launch (start us, length us, event | category | flops | bytes accessed | tf_op | source)
XLA Modules:
  0.0 303.6 jit_solution(1512720498870579981)
XLA Ops:
  6.5 0.0 all-gather.3.cloned.1.call-start
  6.5 0.7 convert_bitcast_fusion
  7.2 0.1 broadcast_bitcast_fusion
  7.3 1.1 multiply_reduce_fusion
  8.4 67.3 %psum.14 = f32[512]{0:T(512)S(1)} all-reduce(f32[512]{0:T(512)S(1)} %multiply_reduce_fusion), channel_id=1, replica_groups=mesh['row'=32,'col'=16] {'row'}, use_global_device_ids=true, to_apply=%region_1.0 | all-reduce | flops 512 | bytes 4096 | tf_op jit(solution)/shard_map/psum | solution.py:30
  75.7 1.8 multiply_convert_fusion
  77.5 0.0 all-gather.3.cloned.1.call-update
  77.5 0.0 all-gather.5.cloned.1.call-start
  77.6 0.7 all-gather.5.cloned.1.call-update
  78.3 77.1 %all-gather.3.cloned.1.call-done = bf16[256,8192]{1,0:T(8,128)(2,1)} async-done(((bf16[256,512]{1,0:T(8,128)(2,1)}), bf16[256,8192]{1,0:T(8,128)(2,1)}) %all-gather.3.cloned.1.call-update) | async-done | bytes 4194320 | tf_op jit(solution)/shard_map/all_gather | solution.py:22
  155.3 68.1 %all-gather.5.cloned.1.call-done = bf16[8192,512]{1,0:T(8,128)(2,1)} async-done(((bf16[256,512]{1,0:T(8,128)(2,1)}), bf16[8192,512]{1,0:T(8,128)(2,1)}) %all-gather.5.cloned.1.call-update) | async-done | bytes 8388624 | tf_op jit(solution)/shard_map/all_gather | solution.py:23
  223.4 7.0 %fusion.1 = (f32[512]{0:T(512)S(1)}, f32[256,512]{1,0:T(8,128)S(1)}) fusion(f32[512]{0:T(512)S(1)} %bitcast.9, bf16[256,8192]{1,0:T(8,128)(2,1)} %all-gather.3.cloned.1.call-done, bf16[8192,512]{1,0:T(8,128)(2,1)} %all-gather.5.cloned.1.call-done), kind=kOutput, calls=%fused_computation.9 | convolution fusion | flops 2147876352 | bytes 13111296 | tf_op jit(solution)/shard_map/dot_general | solution.py:18
  230.4 65.5 %psum.15 = f32[512]{0:T(512)S(1)} all-reduce(f32[512]{0:T(512)S(1)} %get-tuple-element.5), channel_id=1, replica_groups=mesh['row'=32,'col'=16] {'row'}, use_global_device_ids=true, to_apply=%region_3.0 | all-reduce | flops 512 | bytes 4096 | tf_op jit(solution)/shard_map/psum | solution.py:35
  295.9 0.9 broadcast_multiply_fusion
  (3 shorter events, 0.0 us)
Async XLA Ops:
  6.5 148.8 %all-gather.3.cloned.1.call-start = ((), (), s32[]{:S(2)}) async-start(), calls=%async_computation | async-start | bytes 4456448 | tf_op jit(solution)/shard_map/all_gather | solution.py:22
  77.5 145.9 %all-gather.5.cloned.1.call-start = ((), (), s32[]{:S(2)}) async-start(), calls=%async_computation.1 | async-start | bytes 8650752 | tf_op jit(solution)/shard_map/all_gather | solution.py:23
Sparse Core Ops, SparseCore 0:
  77.6 77.6 all-gather.2
  158.5 64.8 all-gather.4
where the time goes:
time: 304 us
  waiting for transfers between devices  146 us (48%)
  blocking collectives  133 us (44%)
  between operations  13.4 us (4%)
  matrix products  6.99 us (2%)
  other arithmetic  4.45 us (1%)
    all_gather x1, waiting for transfers between devices, product(): left = lax.all_gather(operand, 'col', axis=1, tiled=True)  77.1 us
    all_gather x1, waiting for transfers between devices, product(): return tile_sum(left, lax.all_gather(operand, 'row', axis=0, tiled=True))  68.1 us
    psum x1, blocking collectives, shards(): start_total = lax.psum(jnp.sum(held, axis=0), 'row')  67.3 us
    psum x1, blocking collectives, shards(): sums = lax.psum(jnp.sum(inflated, axis=0), 'row')  65.5 us
    dot_general x1, matrix products, tile_sum(): return jnp.dot(left_part, right_part, preferred_element_type=jnp.float32)  6.99 us
  transfers between devices with their start and end apart: 2, of which 2 were waited for; matrix products, arithmetic and copies ran while one was open for 0% of the time, Pallas kernels for 0%

commit v1 on v0

--- a/solution.py
+++ b/solution.py
@@ -19,7 +19,12 @@
 
 
 def product(operand):
-    left = lax.all_gather(operand, "col", axis=1, tiled=True)
+    ring = [operand]
+    for hop in range(15):
+        ring.append(lax.ppermute(ring[-1], "col", [(dev, (dev + 1) % 16) for dev in range(16)]))
+    left = jnp.roll(
+        jnp.concatenate(ring[::-1], axis=1), (lax.axis_index("col") + 1) * ring[0].shape[1], axis=1
+    )
     return tile_sum(left, lax.all_gather(operand, "row", axis=0, tiled=True))
 
 

time: 304 us -> 351 us (1.15)
  the two profiles are of different devices: /device:TPU:32 before, /device:TPU:1 now
where the time goes in v1:
time: 351 us; the launch traced here: 350 us
  blocking collectives  152 us (43%)
  waiting for transfers between devices  113 us (32%)
  local copies, waits for them, and re-layouts  29.6 us (8%)
  starting transfers between devices  28.6 us (8%)
  between operations  13.6 us (4%)
  matrix products  7 us (2%)
  other arithmetic  6.07 us (2%)
    ppermute x15, waiting for transfers between devices, product(): lax.ppermute(ring[-1], 'col', [(dev, (dev + 1) % 16) for dev in range(16)])  113 us
    psum x1, blocking collectives, shards(): sums = lax.psum(jnp.sum(inflated, axis=0), 'row')  82.9 us
    psum x1, blocking collectives, shards(): start_total = lax.psum(jnp.sum(held, axis=0), 'row')  68.9 us
    unnamed x42, local copies, waits for them, and re-layouts  29.6 us
    ppermute x15, starting transfers between devices, product(): lax.ppermute(ring[-1], 'col', [(dev, (dev + 1) % 16) for dev in range(16)])  28.6 us
  transfers between devices with their start and end apart: 16, of which 15 were waited for; matrix products, arithmetic and copies ran while one was open for 8% of the time, Pallas kernels for 0%

profile of v1, /device:TPU:1, one launch (start us, length us, event | category | flops | bytes accessed | tf_op | source)
XLA Modules:
  0.0 349.8 jit_solution(1014179625667337575)
XLA Ops:
  7.3 1.1 multiply_reduce_fusion
  8.4 68.9 %psum.14 = f32[512]{0:T(512)S(1)} all-reduce(f32[512]{0:T(512)S(1)} %multiply_reduce_fusion), channel_id=1, replica_groups=mesh['row'=32,'col'=16] {'row'}, use_global_device_ids=true, to_apply=%region_1.0 | all-reduce | flops 512 | bytes 4096 | tf_op jit(solution)/shard_map/psum | solution.py:35
  77.3 1.8 multiply_convert_fusion
  79.2 1.9 collective-permute-start
  81.1 8.0 %collective-permute-done = bf16[256,512]{1,0:T(8,128)(2,1)S(1)} collective-permute-done((bf16[256,512]{1,0:T(8,128)(2,1)}, bf16[256,512]{1,0:T(8,128)(2,1)S(1)}, u32[]{:S(2)}, u32[]{:S(2)}) %collective-permute-start) | collective-permute-done | bytes 262176 | tf_op jit(solution)/shard_map/ppermute | solution.py:24
  89.2 1.9 collective-permute-start.1
  91.1 6.4 %collective-permute-done.1 = bf16[256,512]{1,0:T(8,128)(2,1)S(1)} collective-permute-done((bf16[256,512]{1,0:T(8,128)(2,1)S(1)}, bf16[256,512]{1,0:T(8,128)(2,1)S(1)}, u32[]{:S(2)}, u32[]{:S(2)}) %collective-permute-start.1) | collective-permute-done | bytes 262176 | tf_op jit(solution)/shard_map/ppermute | solution.py:24
  97.5 1.9 collective-permute-start.2
  99.4 7.2 %collective-permute-done.2 = bf16[256,512]{1,0:T(8,128)(2,1)S(1)} collective-permute-done((bf16[256,512]{1,0:T(8,128)(2,1)S(1)}, bf16[256,512]{1,0:T(8,128)(2,1)S(1)}, u32[]{:S(2)}, u32[]{:S(2)}) %collective-permute-start.2) | collective-permute-done | bytes 262176 | tf_op jit(solution)/shard_map/ppermute | solution.py:24
  106.6 1.9 collective-permute-start.3
  108.5 8.6 %collective-permute-done.3 = bf16[256,512]{1,0:T(8,128)(2,1)S(1)} collective-permute-done((bf16[256,512]{1,0:T(8,128)(2,1)S(1)}, bf16[256,512]{1,0:T(8,128)(2,1)S(1)}, u32[]{:S(2)}, u32[]{:S(2)}) %collective-permute-start.3) | collective-permute-done | bytes 262176 | tf_op jit(solution)/shard_map/ppermute | solution.py:24
  117.1 1.9 collective-permute-start.4
  119.0 9.1 %collective-permute-done.4 = bf16[256,512]{1,0:T(8,128)(2,1)S(1)} collective-permute-done((bf16[256,512]{1,0:T(8,128)(2,1)S(1)}, bf16[256,512]{1,0:T(8,128)(2,1)S(1)}, u32[]{:S(2)}, u32[]{:S(2)}) %collective-permute-start.4) | collective-permute-done | bytes 262176 | tf_op jit(solution)/shard_map/ppermute | solution.py:24
  128.1 1.9 collective-permute-start.5
  130.0 8.2 %collective-permute-done.5 = bf16[256,512]{1,0:T(8,128)(2,1)S(1)} collective-permute-done((bf16[256,512]{1,0:T(8,128)(2,1)S(1)}, bf16[256,512]{1,0:T(8,128)(2,1)S(1)}, u32[]{:S(2)}, u32[]{:S(2)}) %collective-permute-start.5) | collective-permute-done | bytes 262176 | tf_op jit(solution)/shard_map/ppermute | solution.py:24
  138.2 1.9 collective-permute-start.6
  140.2 7.3 %collective-permute-done.6 = bf16[256,512]{1,0:T(8,128)(2,1)S(1)} collective-permute-done((bf16[256,512]{1,0:T(8,128)(2,1)S(1)}, bf16[256,512]{1,0:T(8,128)(2,1)S(1)}, u32[]{:S(2)}, u32[]{:S(2)}) %collective-permute-start.6) | collective-permute-done | bytes 262176 | tf_op jit(solution)/shard_map/ppermute | solution.py:24
  147.5 1.9 collective-permute-start.7
  149.4 6.4 %collective-permute-done.7 = bf16[256,512]{1,0:T(8,128)(2,1)S(1)} collective-permute-done((bf16[256,512]{1,0:T(8,128)(2,1)S(1)}, bf16[256,512]{1,0:T(8,128)(2,1)S(1)}, u32[]{:S(2)}, u32[]{:S(2)}) %collective-permute-start.7) | collective-permute-done | bytes 262176 | tf_op jit(solution)/shard_map/ppermute | solution.py:24
  155.8 1.9 collective-permute-start.8
  157.7 6.4 %collective-permute-done.8 = bf16[256,512]{1,0:T(8,128)(2,1)S(1)} collective-permute-done((bf16[256,512]{1,0:T(8,128)(2,1)S(1)}, bf16[256,512]{1,0:T(8,128)(2,1)S(1)}, u32[]{:S(2)}, u32[]{:S(2)}) %collective-permute-start.8) | collective-permute-done | bytes 262176 | tf_op jit(solution)/shard_map/ppermute | solution.py:24
  164.1 1.9 collective-permute-start.9
  166.0 6.4 %collective-permute-done.9 = bf16[256,512]{1,0:T(8,128)(2,1)S(1)} collective-permute-done((bf16[256,512]{1,0:T(8,128)(2,1)S(1)}, bf16[256,512]{1,0:T(8,128)(2,1)S(1)}, u32[]{:S(2)}, u32[]{:S(2)}) %collective-permute-start.9) | collective-permute-done | bytes 262176 | tf_op jit(solution)/shard_map/ppermute | solution.py:24
  172.4 1.9 collective-permute-start.10
  174.3 6.4 %collective-permute-done.10 = bf16[256,512]{1,0:T(8,128)(2,1)S(1)} collective-permute-done((bf16[256,512]{1,0:T(8,128)(2,1)S(1)}, bf16[256,512]{1,0:T(8,128)(2,1)S(1)}, u32[]{:S(2)}, u32[]{:S(2)}) %collective-permute-start.10) | collective-permute-done | bytes 262176 | tf_op jit(solution)/shard_map/ppermute | solution.py:24
  180.7 1.9 collective-permute-start.11
  182.7 7.4 %collective-permute-done.11 = bf16[256,512]{1,0:T(8,128)(2,1)S(1)} collective-permute-done((bf16[256,512]{1,0:T(8,128)(2,1)S(1)}, bf16[256,512]{1,0:T(8,128)(2,1)S(1)}, u32[]{:S(2)}, u32[]{:S(2)}) %collective-permute-start.11) | collective-permute-done | bytes 262176 | tf_op jit(solution)/shard_map/ppermute | solution.py:24
  190.8 1.9 collective-permute-start.12
  192.7 7.8 %collective-permute-done.12 = bf16[256,512]{1,0:T(8,128)(2,1)S(1)} collective-permute-done((bf16[256,512]{1,0:T(8,128)(2,1)S(1)}, bf16[256,512]{1,0:T(8,128)(2,1)S(1)}, u32[]{:S(2)}, u32[]{:S(2)}) %collective-permute-start.12) | collective-permute-done | bytes 262176 | tf_op jit(solution)/shard_map/ppermute | solution.py:24
  201.1 1.9 collective-permute-start.13
  203.0 8.2 %collective-permute-done.13 = bf16[256,512]{1,0:T(8,128)(2,1)} collective-permute-done((bf16[256,512]{1,0:T(8,128)(2,1)S(1)}, bf16[256,512]{1,0:T(8,128)(2,1)}, u32[]{:S(2)}, u32[]{:S(2)}) %collective-permute-start.13) | collective-permute-done | bytes 262176 | tf_op jit(solution)/shard_map/ppermute | solution.py:24
  211.3 1.9 collective-permute-start.14
  213.2 9.3 %collective-permute-done.14 = bf16[256,512]{1,0:T(8,128)(2,1)} collective-permute-done((bf16[256,512]{1,0:T(8,128)(2,1)}, bf16[256,512]{1,0:T(8,128)(2,1)}, u32[]{:S(2)}, u32[]{:S(2)}) %collective-permute-start.14) | collective-permute-done | bytes 262176 | tf_op jit(solution)/shard_map/ppermute | solution.py:24
  222.5 1.7 constant_dynamic-update-slice_fusion.31
  224.2 1.7 constant_dynamic-update-slice_fusion.30
  225.9 1.7 constant_dynamic-update-slice_fusion.29
  227.6 1.7 constant_dynamic-update-slice_fusion.28
  234.5 0.8 constant_dynamic-update-slice_fusion.20
  235.3 0.8 constant_dynamic-update-slice_fusion.19
  237.5 0.8 constant_dynamic-update-slice_fusion.16
  238.3 1.7 constant_dynamic-update-slice_fusion.15
  240.0 1.7 constant_dynamic-update-slice_fusion.14
  243.2 0.8 constant_dynamic-update-slice_fusion.11
  243.9 0.8 constant_dynamic-update-slice_fusion.10
  251.4 0.8 constant_dynamic-update-slice_fusion
  252.2 7.0 %fusion.9 = (f32[512]{0:T(512)S(1)}, f32[256,512]{1,0:T(8,128)S(1)}) fusion(f32[512]{0:T(512)S(1)} %bitcast.10, bf16[8192,512]{1,0:T(8,128)(2,1)} %all-gather.2.cloned.1.call-done, bf16[256,16384]{1,0:T(8,128)(2,1)} %constant_dynamic-update-slice_fusion, s32[]{:T(128)S(6)} %select_n.14), kind=kOutput, calls=%fused_computation.44 | convolution fusion | flops 2147876352 | bytes 13111300 | tf_op jit(solution)/shard_map/dot_general | solution.py:18
  259.2 82.9 %psum.15 = f32[512]{0:T(512)S(1)} all-reduce(f32[512]{0:T(512)S(1)} %get-tuple-element.5), channel_id=1, replica_groups=mesh['row'=32,'col'=16] {'row'}, use_global_device_ids=true, to_apply=%region_3.4 | all-reduce | flops 512 | bytes 4096 | tf_op jit(solution)/shard_map/psum | solution.py:40
  342.1 0.9 broadcast_multiply_fusion
  (38 shorter events, 17.1 us)
Async XLA Ops:
  6.5 231.0 %copy-start = (f32[256,512]{1,0:T(8,128)S(1)}, f32[256,512]{1,0:T(8,128)}, u32[]{:S(2)}) copy-start(f32[256,512]{1,0:T(8,128)} %param.2) | copy-start | bytes 1572868
  6.5 245.7 %all-gather.2.cloned.1.call-start = ((), (), s32[]{:S(2)}) async-start(), calls=%async_computation | async-start | bytes 8650752 | tf_op jit(solution)/shard_map/all_gather | solution.py:28
  79.2 10.0 %collective-permute-start = (bf16[256,512]{1,0:T(8,128)(2,1)}, bf16[256,512]{1,0:T(8,128)(2,1)S(1)}, u32[]{:S(2)}, u32[]{:S(2)}) collective-permute-start(bf16[256,512]{1,0:T(8,128)(2,1)} %multiply_convert_fusion), channel_id=1, source_target_pairs={{0,1},{1,2},{2,3},{3,4},{4,5},{5,6},{6,7},{7,8},{8,9},{9,10},{10,1... | collective-permute-start | bytes 786440 | tf_op jit(solution)/shard_map/ppermute | solution.py:24
  89.2 8.3 %collective-permute-start.1 = (bf16[256,512]{1,0:T(8,128)(2,1)S(1)}, bf16[256,512]{1,0:T(8,128)(2,1)S(1)}, u32[]{:S(2)}, u32[]{:S(2)}) collective-permute-start(bf16[256,512]{1,0:T(8,128)(2,1)S(1)} %collective-permute-done), channel_id=1, source_target_pairs={{0,1},{1,2},{2,3},{3,4},{4,5},{5,6},{6,7},{7,8},{8,9},{9,10},{10,1... | collective-permute-start | bytes 786440 | tf_op jit(solution)/shard_map/ppermute | solution.py:24
  97.5 9.2 %collective-permute-start.2 = (bf16[256,512]{1,0:T(8,128)(2,1)S(1)}, bf16[256,512]{1,0:T(8,128)(2,1)S(1)}, u32[]{:S(2)}, u32[]{:S(2)}) collective-permute-start(bf16[256,512]{1,0:T(8,128)(2,1)S(1)} %collective-permute-done.1), channel_id=1, source_target_pairs={{0,1},{1,2},{2,3},{3,4},{4,5},{5,6},{6,7},{7,8},{8,9},{9,10},{10,1... | collective-permute-start | bytes 786440 | tf_op jit(solution)/shard_map/ppermute | solution.py:24
  106.6 10.5 %collective-permute-start.3 = (bf16[256,512]{1,0:T(8,128)(2,1)S(1)}, bf16[256,512]{1,0:T(8,128)(2,1)S(1)}, u32[]{:S(2)}, u32[]{:S(2)}) collective-permute-start(bf16[256,512]{1,0:T(8,128)(2,1)S(1)} %collective-permute-done.2), channel_id=1, source_target_pairs={{0,1},{1,2},{2,3},{3,4},{4,5},{5,6},{6,7},{7,8},{8,9},{9,10},{10,1... | collective-permute-start | bytes 786440 | tf_op jit(solution)/shard_map/ppermute | solution.py:24
  117.1 11.0 %collective-permute-start.4 = (bf16[256,512]{1,0:T(8,128)(2,1)S(1)}, bf16[256,512]{1,0:T(8,128)(2,1)S(1)}, u32[]{:S(2)}, u32[]{:S(2)}) collective-permute-start(bf16[256,512]{1,0:T(8,128)(2,1)S(1)} %collective-permute-done.3), channel_id=1, source_target_pairs={{0,1},{1,2},{2,3},{3,4},{4,5},{5,6},{6,7},{7,8},{8,9},{9,10},{10,1... | collective-permute-start | bytes 786440 | tf_op jit(solution)/shard_map/ppermute | solution.py:24
  128.1 10.1 %collective-permute-start.5 = (bf16[256,512]{1,0:T(8,128)(2,1)S(1)}, bf16[256,512]{1,0:T(8,128)(2,1)S(1)}, u32[]{:S(2)}, u32[]{:S(2)}) collective-permute-start(bf16[256,512]{1,0:T(8,128)(2,1)S(1)} %collective-permute-done.4), channel_id=1, source_target_pairs={{0,1},{1,2},{2,3},{3,4},{4,5},{5,6},{6,7},{7,8},{8,9},{9,10},{10,1... | collective-permute-start | bytes 786440 | tf_op jit(solution)/shard_map/ppermute | solution.py:24
  138.2 9.2 %collective-permute-start.6 = (bf16[256,512]{1,0:T(8,128)(2,1)S(1)}, bf16[256,512]{1,0:T(8,128)(2,1)S(1)}, u32[]{:S(2)}, u32[]{:S(2)}) collective-permute-start(bf16[256,512]{1,0:T(8,128)(2,1)S(1)} %collective-permute-done.5), channel_id=1, source_target_pairs={{0,1},{1,2},{2,3},{3,4},{4,5},{5,6},{6,7},{7,8},{8,9},{9,10},{10,1... | collective-permute-start | bytes 786440 | tf_op jit(solution)/shard_map/ppermute | solution.py:24
  147.5 8.3 %collective-permute-start.7 = (bf16[256,512]{1,0:T(8,128)(2,1)S(1)}, bf16[256,512]{1,0:T(8,128)(2,1)S(1)}, u32[]{:S(2)}, u32[]{:S(2)}) collective-permute-start(bf16[256,512]{1,0:T(8,128)(2,1)S(1)} %collective-permute-done.6), channel_id=1, source_target_pairs={{0,1},{1,2},{2,3},{3,4},{4,5},{5,6},{6,7},{7,8},{8,9},{9,10},{10,1... | collective-permute-start | bytes 786440 | tf_op jit(solution)/shard_map/ppermute | solution.py:24
  155.8 8.3 %collective-permute-start.8 = (bf16[256,512]{1,0:T(8,128)(2,1)S(1)}, bf16[256,512]{1,0:T(8,128)(2,1)S(1)}, u32[]{:S(2)}, u32[]{:S(2)}) collective-permute-start(bf16[256,512]{1,0:T(8,128)(2,1)S(1)} %collective-permute-done.7), channel_id=1, source_target_pairs={{0,1},{1,2},{2,3},{3,4},{4,5},{5,6},{6,7},{7,8},{8,9},{9,10},{10,1... | collective-permute-start | bytes 786440 | tf_op jit(solution)/shard_map/ppermute | solution.py:24
  164.1 8.3 %collective-permute-start.9 = (bf16[256,512]{1,0:T(8,128)(2,1)S(1)}, bf16[256,512]{1,0:T(8,128)(2,1)S(1)}, u32[]{:S(2)}, u32[]{:S(2)}) collective-permute-start(bf16[256,512]{1,0:T(8,128)(2,1)S(1)} %collective-permute-done.8), channel_id=1, source_target_pairs={{0,1},{1,2},{2,3},{3,4},{4,5},{5,6},{6,7},{7,8},{8,9},{9,10},{10,1... | collective-permute-start | bytes 786440 | tf_op jit(solution)/shard_map/ppermute | solution.py:24
  172.4 8.3 %collective-permute-start.10 = (bf16[256,512]{1,0:T(8,128)(2,1)S(1)}, bf16[256,512]{1,0:T(8,128)(2,1)S(1)}, u32[]{:S(2)}, u32[]{:S(2)}) collective-permute-start(bf16[256,512]{1,0:T(8,128)(2,1)S(1)} %collective-permute-done.9), channel_id=1, source_target_pairs={{0,1},{1,2},{2,3},{3,4},{4,5},{5,6},{6,7},{7,8},{8,9},{9,10},{10,1... | collective-permute-start | bytes 786440 | tf_op jit(solution)/shard_map/ppermute | solution.py:24
  180.7 9.3 %collective-permute-start.11 = (bf16[256,512]{1,0:T(8,128)(2,1)S(1)}, bf16[256,512]{1,0:T(8,128)(2,1)S(1)}, u32[]{:S(2)}, u32[]{:S(2)}) collective-permute-start(bf16[256,512]{1,0:T(8,128)(2,1)S(1)} %collective-permute-done.10), channel_id=1, source_target_pairs={{0,1},{1,2},{2,3},{3,4},{4,5},{5,6},{6,7},{7,8},{8,9},{9,10},{10,1... | collective-permute-start | bytes 786440 | tf_op jit(solution)/shard_map/ppermute | solution.py:24
  190.0 0.7 copy-start.1
  190.8 9.7 %collective-permute-start.12 = (bf16[256,512]{1,0:T(8,128)(2,1)S(1)}, bf16[256,512]{1,0:T(8,128)(2,1)S(1)}, u32[]{:S(2)}, u32[]{:S(2)}) collective-permute-start(bf16[256,512]{1,0:T(8,128)(2,1)S(1)} %collective-permute-done.11), channel_id=1, source_target_pairs={{0,1},{1,2},{2,3},{3,4},{4,5},{5,6},{6,7},{7,8},{8,9},{9,10},{10,1... | collective-permute-start | bytes 786440 | tf_op jit(solution)/shard_map/ppermute | solution.py:24
  200.4 0.7 copy-start.3
  201.1 10.2 %collective-permute-start.13 = (bf16[256,512]{1,0:T(8,128)(2,1)S(1)}, bf16[256,512]{1,0:T(8,128)(2,1)}, u32[]{:S(2)}, u32[]{:S(2)}) collective-permute-start(bf16[256,512]{1,0:T(8,128)(2,1)S(1)} %collective-permute-done.12), channel_id=1, source_target_pairs={{0,1},{1,2},{2,3},{3,4},{4,5},{5,6},{6,7},{7,8},{8,9},{9,10},{10,1... | collective-permute-start | bytes 786440 | tf_op jit(solution)/shard_map/ppermute | solution.py:24
  211.3 11.2 %collective-permute-start.14 = (bf16[256,512]{1,0:T(8,128)(2,1)}, bf16[256,512]{1,0:T(8,128)(2,1)}, u32[]{:S(2)}, u32[]{:S(2)}) collective-permute-start(bf16[256,512]{1,0:T(8,128)(2,1)} %collective-permute-done.13), channel_id=1, source_target_pairs={{0,1},{1,2},{2,3},{3,4},{4,5},{5,6},{6,7},{7,8},{8,9},{9,10},{10,1... | collective-permute-start | bytes 786440 | tf_op jit(solution)/shard_map/ppermute | solution.py:24
  213.2 28.4 %copy-start.4 = (bf16[256,512]{1,0:T(8,128)(2,1)S(1)}, bf16[256,512]{1,0:T(8,128)(2,1)}, u32[]{:S(2)}) copy-start(bf16[256,512]{1,0:T(8,128)(2,1)} %copy-done.3) | copy-start | bytes 786436
  213.2 29.2 %copy-start.2 = (bf16[256,512]{1,0:T(8,128)(2,1)S(1)}, bf16[256,512]{1,0:T(8,128)(2,1)}, u32[]{:S(2)}) copy-start(bf16[256,512]{1,0:T(8,128)(2,1)} %copy-done.1) | copy-start | bytes 786436
Sparse Core Ops, SparseCore 0:
  79.3 67.2 all-gather.1

commit v2 on v0

--- a/solution.py
+++ b/solution.py
@@ -32,7 +32,7 @@
     operand = matrix.astype(jnp.bfloat16)
     expanded = product(operand) * cells
     inflated = expanded * expanded
-    sums = lax.psum(jnp.sum(inflated, axis=0), "row")
+    sums = jnp.sum(lax.all_gather(jnp.sum(inflated, axis=0), "row"), axis=0)
     matrix = inflated * (total_rows / sums)[None, :]
     return matrix
 

time: 304 us -> 264 us (0.87)
  the two profiles are of different devices: /device:TPU:32 before, /device:TPU:1 now
where the time goes in v2:
time: 264 us
  waiting for transfers between devices  146 us (55%)
  blocking collectives  92.8 us (35%)
  between operations  13.4 us (5%)
  matrix products  7 us (3%)
  other arithmetic  4.51 us (2%)
    all_gather x1, waiting for transfers between devices, product(): return tile_sum(left, lax.all_gather(operand, 'row', axis=0, tiled=True))  77.2 us
    psum x1, blocking collectives, shards(): start_total = lax.psum(jnp.sum(held, axis=0), 'row')  68.9 us
    all_gather x1, waiting for transfers between devices, product(): left = lax.all_gather(operand, 'col', axis=1, tiled=True)  68 us
    all_gather x1, blocking collectives, shards(): sums = jnp.sum(lax.all_gather(jnp.sum(inflated, axis=0), 'row'), axis=0)  23.9 us
    dot_general x1, matrix products, tile_sum(): return jnp.dot(left_part, right_part, preferred_element_type=jnp.float32)  7 us
  transfers between devices with their start and end apart: 2, of which 2 were waited for; matrix products, arithmetic and copies ran while one was open for 0% of the time, Pallas kernels for 0%

profile of v2, /device:TPU:1, one launch (start us, length us, event | category | flops | bytes accessed | tf_op | source)
XLA Modules:
  0.0 263.7 jit_solution(3359226580402586293)
XLA Ops:
  6.5 0.0 all-gather.5.cloned.1.call-start
  6.5 0.7 convert_bitcast_fusion
  7.2 0.1 broadcast_bitcast_fusion
  7.3 1.1 multiply_reduce_fusion
  8.4 68.9 %psum.7 = f32[512]{0:T(512)S(1)} all-reduce(f32[512]{0:T(512)S(1)} %multiply_reduce_fusion), channel_id=1, replica_groups=mesh['row'=32,'col'=16] {'row'}, use_global_device_ids=true, to_apply=%region_1.0 | all-reduce | flops 512 | bytes 4096 | tf_op jit(solution)/shard_map/psum | solution.py:30
  77.3 1.8 multiply_convert_fusion
  79.1 0.0 all-gather.5.cloned.1.call-update
  79.1 0.0 all-gather.7.cloned.1.call-start
  79.2 0.7 all-gather.7.cloned.1.call-update
  79.9 68.0 %all-gather.5.cloned.1.call-done = bf16[256,8192]{1,0:T(8,128)(2,1)} async-done(((bf16[256,512]{1,0:T(8,128)(2,1)}), bf16[256,8192]{1,0:T(8,128)(2,1)}) %all-gather.5.cloned.1.call-update) | async-done | bytes 4194320 | tf_op jit(solution)/shard_map/all_gather | solution.py:22
  147.8 77.2 %all-gather.7.cloned.1.call-done = bf16[8192,512]{1,0:T(8,128)(2,1)} async-done(((bf16[256,512]{1,0:T(8,128)(2,1)}), bf16[8192,512]{1,0:T(8,128)(2,1)}) %all-gather.7.cloned.1.call-update) | async-done | bytes 8388624 | tf_op jit(solution)/shard_map/all_gather | solution.py:23
  225.0 7.0 %fusion.1 = (f32[512]{0:T(512)S(1)}, f32[256,512]{1,0:T(8,128)S(1)}) fusion(f32[512]{0:T(512)S(1)} %bitcast.10, bf16[256,8192]{1,0:T(8,128)(2,1)} %all-gather.5.cloned.1.call-done, bf16[8192,512]{1,0:T(8,128)(2,1)} %all-gather.7.cloned.1.call-done), kind=kOutput, calls=%fused_computation.9 | convolution fusion | flops 2147876352 | bytes 13111296 | tf_op jit(solution)/shard_map/dot_general | solution.py:18
  232.0 23.9 %all-gather.1 = f32[32,1,512]{2,1,0:T(1,128)S(1)} all-gather(f32[1,1,512]{2,1,0:T(1,128)S(1)} %bitcast.11), channel_id=2, replica_groups=mesh['row'=32,'col'=16] {'row'}, dimensions={0}, use_global_device_ids=true | all-gather | bytes 67584 | tf_op jit(solution)/shard_map/all_gather | solution.py:35
  255.9 0.1 reduce_sum.29
  256.0 0.9 broadcast_multiply_fusion
  (3 shorter events, 0.0 us)
Async XLA Ops:
  6.5 141.3 %all-gather.5.cloned.1.call-start = ((), (), s32[]{:S(2)}) async-start(), calls=%async_computation | async-start | bytes 4456448 | tf_op jit(solution)/shard_map/all_gather | solution.py:22
  79.1 145.9 %all-gather.7.cloned.1.call-start = ((), (), s32[]{:S(2)}) async-start(), calls=%async_computation.1 | async-start | bytes 8650752 | tf_op jit(solution)/shard_map/all_gather | solution.py:23
Sparse Core Ops, SparseCore 0:
  79.2 68.5 all-gather.4
  151.0 73.9 all-gather.6
